TPU v7x, 32 devices: a whole 2x2x4 slice. The times are simulated.
32 devices in a mesh: parts: 2 (over y), cell: 4 (over z), grp: 4 (over x, core).
Axes of the slice: x: 2, y: 2, z: 4, core: 2. Of those that a mesh axis runs over, the one named last changes fastest.
Arguments:
- sketch: bfloat16 [98304, 256], P(('parts', 'cell', 'grp')), parts along dimension 0, may hold values from -0.27063294 to 0.27063294, as said below
- slab: bfloat16 [98304, 128], P(('parts', 'cell', 'grp')), parts along dimension 0, may hold values from -6 to 6
Outputs:
- r_factor: float32 [512, 256], P('parts'), parts along dimension 0
- basis: bfloat16 [98304, 256], P(('parts', 'cell', 'grp')), parts along dimension 0
- projected: float32 [512, 128], P(('parts', 'cell'), 'grp'), parts along dimension 0
There are 2 independent parts, one for each index of `parts`. A program takes and returns all parts, laid end to end along the dimension named above; each array names one. Nothing has to cross between parts.
Inputs may be any that keep to these rules, and one draw needn't show every extreme that they name: A scaled random sketch of full column rank.
All inputs are finite; a program needn't handle non-finite values.
Results may differ from a plain program's by a relative error of at most 0.001.
Values sent between devices are 32-bit elements; how exact they have to be, the bound alone decides.
A program may use at most 64 MiB of HBM per device.

v0:
```python
import functools

import jax
import jax.numpy as jnp
from jax import lax
from jax.experimental import pallas as pl
from jax.experimental.pallas import tpu as pltpu
from jax.sharding import PartitionSpec as P

SUB = 8
BASE = 64
SUM_STEP = 768
BASIS_STEP = 512
HIGHEST = lax.Precision.HIGHEST


def dot(a, b, contract, precision=None):
    return lax.dot_general(
        a, b, (contract, ((), ())), precision=precision, preferred_element_type=jnp.float32
    )


def chunks_of(total, step):
    return [pl.ds(start, min(step, total - start)) for start in range(0, total, step)]


def sums_over(a_ref, b_ref, loads):
    total = None
    for rows, load in loads:
        load.wait()
        part = dot(a_ref[rows, :], b_ref[rows, :], ((0,), (0,)))
        total = part if total is None else total + part
    return total


def reduce_kernel(
    cells, grps, sketch_hbm, slab_hbm, gram_ref, cross_ref,
    sketch_ref, slab_ref, sketch_sems, slab_sems,
    own_gram, own_cross, grp_gram, grp_cross, cell_gram, cell_cross,
    gs_send, gs_recv, cs_send, cs_recv, gz_send, gz_recv, cz_send, cz_recv, ag_send, ag_recv,
):
    def loading(source, target, sems):
        loads = []
        for i, rows in enumerate(chunks_of(source.shape[0], SUM_STEP)):
            load = pltpu.make_async_copy(source.at[rows, :], target.at[rows, :], sems.at[i])
            load.start()
            loads.append((rows, load))
        return loads

    sketch_loads = loading(sketch_hbm, sketch_ref, sketch_sems)
    slab_loads = loading(slab_hbm, slab_ref, slab_sems)
    me_c = lax.axis_index("cell")
    me_g = lax.axis_index("grp")
    half = own_gram.shape[1]
    gram_rows = own_gram.shape[0] // grps
    cross_rows = own_cross.shape[0] // grps
    days = cross_rows // 2

    barrier = pltpu.get_barrier_semaphore()
    for d in range(1, grps):
        pl.semaphore_signal(barrier, inc=1, device_id={"grp": lax.rem(me_g + d, grps)}, device_id_type=pl.DeviceIdType.MESH)
    for d in range(1, cells):
        pl.semaphore_signal(barrier, inc=1, device_id={"cell": lax.rem(me_c + d, cells)}, device_id_type=pl.DeviceIdType.MESH)

    gram = sums_over(sketch_ref, sketch_ref, sketch_loads)
    own_gram[0:half, :] = gram[:half, :half]
    own_gram[half : 2 * half, :] = gram[:half, half:]
    own_gram[2 * half :, :] = gram[half:, half:]
    pl.semaphore_wait(barrier, grps + cells - 2)

    def rows_of(ref, index, count):
        return ref.at[pl.ds(pl.multiple_of(index * count, SUB), count), :]

    def to_grps(own, landing, count, send, recv):
        copies = []
        for d in range(1, grps):
            peer = lax.rem(me_g + d, grps)
            copies.append(pltpu.make_async_remote_copy(
                src_ref=rows_of(own, peer, count), dst_ref=landing.at[d - 1],
                send_sem=send.at[d - 1], recv_sem=recv.at[d - 1],
                device_id={"grp": peer}, device_id_type=pl.DeviceIdType.MESH))
        for copy in copies:
            copy.start()
        return copies

    def to_cells(slots, send, recv):
        copies = []
        for d in range(1, cells):
            peer = lax.rem(me_c + d, cells)
            copies.append(pltpu.make_async_remote_copy(
                src_ref=slots.at[me_c], dst_ref=slots.at[me_c],
                send_sem=send.at[d - 1], recv_sem=recv.at[d - 1],
                device_id={"cell": peer}, device_id_type=pl.DeviceIdType.MESH))
        for copy in copies:
            copy.start()
        return copies

    gs = to_grps(own_gram, grp_gram, gram_rows, gs_send, gs_recv)

    cross = sums_over(slab_ref, sketch_ref, slab_loads)
    for g in range(grps):
        own_cross[g * cross_rows : g * cross_rows + days, :] = cross[g * days : (g + 1) * days, :half]
        own_cross[g * cross_rows + days : (g + 1) * cross_rows, :] = cross[g * days : (g + 1) * days, half:]
    cs = to_grps(own_cross, grp_cross, cross_rows, cs_send, cs_recv)

    def sum_grps(copies, own, landing, count, slots):
        for copy in copies:
            copy.wait_recv()
        total = own[pl.ds(pl.multiple_of(me_g * count, SUB), count), :]
        for d in range(1, grps):
            total = total + landing[d - 1]
        slots[me_c] = total

    sum_grps(gs, own_gram, grp_gram, gram_rows, cell_gram)
    gz = to_cells(cell_gram, gz_send, gz_recv)
    sum_grps(cs, own_cross, grp_cross, cross_rows, cell_cross)
    cz = to_cells(cell_cross, cz_send, cz_recv)

    def sum_cells(copies, slots):
        for copy in copies:
            copy.wait_recv()
        total = slots[0]
        for c in range(1, cells):
            total = total + slots[c]
        return total

    gram_ref[pl.ds(pl.multiple_of(me_g * gram_rows, SUB), gram_rows), :] = sum_cells(gz, cell_gram)
    ag = []
    for d in range(1, grps):
        own = rows_of(gram_ref, me_g, gram_rows)
        ag.append(pltpu.make_async_remote_copy(
            src_ref=own, dst_ref=own, send_sem=ag_send.at[d - 1], recv_sem=ag_recv.at[d - 1],
            device_id={"grp": lax.rem(me_g + d, grps)}, device_id_type=pl.DeviceIdType.MESH))
    for copy in ag:
        copy.start()
    cross_ref[...] = sum_cells(cz, cell_cross)
    for copy in ag:
        copy.wait_recv()
    for copy in gs + cs + gz + cz + ag:
        copy.wait_send()


def reduced(sketch, slab, cells, grps):
    k, days = sketch.shape[1], slab.shape[1]
    half = k // 2
    gram_rows, cross_rows = 3 * half // grps, 2 * days // grps
    if gram_rows % SUB or cross_rows % (2 * SUB) or 3 * half % grps or grps < 2 or cells < 2:
        gram, cross = lax.psum((dot(sketch, sketch, ((0,), (0,))), dot(slab, sketch, ((0,), (0,)))), ("cell", "grp"))
        blocks = jnp.concatenate([gram[:half, :half], gram[:half, half:], gram[half:, half:]], axis=0)
        width = days // grps
        mine = lax.dynamic_slice(cross, (lax.axis_index("grp") * width, 0), (width, k))
        return blocks, jnp.concatenate([mine[:, :half], mine[:, half:]], axis=0)
    f32 = jnp.float32
    dma = pltpu.SemaphoreType.DMA
    return pl.pallas_call(
        functools.partial(reduce_kernel, cells, grps),
        out_shape=(jax.ShapeDtypeStruct((3 * half, half), f32), jax.ShapeDtypeStruct((cross_rows, half), f32)),
        in_specs=[pl.BlockSpec(memory_space=pl.ANY)] * 2,
        out_specs=(pl.BlockSpec(memory_space=pltpu.VMEM),) * 2,
        scratch_shapes=[
            pltpu.VMEM(sketch.shape, sketch.dtype),
            pltpu.VMEM(slab.shape, slab.dtype),
            dma((len(chunks_of(sketch.shape[0], SUM_STEP)),)),
            dma((len(chunks_of(slab.shape[0], SUM_STEP)),)),
            pltpu.VMEM((3 * half, half), f32),
            pltpu.VMEM((2 * days, half), f32),
            pltpu.VMEM((grps - 1, gram_rows, half), f32),
            pltpu.VMEM((grps - 1, cross_rows, half), f32),
            pltpu.VMEM((cells, gram_rows, half), f32),
            pltpu.VMEM((cells, cross_rows, half), f32),
        ] + [dma((grps - 1,))] * 4 + [dma((cells - 1,))] * 4 + [dma((grps - 1,))] * 2,
        compiler_params=pltpu.CompilerParams(collective_id=0, has_side_effects=True),
        name="reduce_sums",
    )(sketch, slab)


def tree(terms):
    while len(terms) > 1:
        terms = [a + b for a, b in zip(terms[::2], terms[1::2])]
    return terms[0]


def factor_base(block, ones_ref):
    n = block.shape[0]
    shape = (SUB, 2 * n)
    ones = ones_ref[:, : 2 * n]
    tiles = n // SUB
    sub = lax.broadcasted_iota(jnp.int32, shape, 0)
    lane = lax.broadcasted_iota(jnp.int32, shape, 1)
    eye = jnp.where(
        lax.broadcasted_iota(jnp.int32, (n, n), 0) == lax.broadcasted_iota(jnp.int32, (n, n), 1), 1.0, 0.0)
    wide = jnp.concatenate([block, eye.astype(jnp.float32)], axis=1)
    m = [wide[q * SUB : (q + 1) * SUB, :] for q in range(tiles)]
    done = []

    def row(x, j):
        return jnp.broadcast_to(x[j : j + 1, :], shape)

    def col(x, j):
        return jnp.broadcast_to(x[:, j : j + 1], shape)

    for p in range(tiles):
        t = m[p]
        c = [col(t, p * SUB + i) * ones for i in range(SUB)]
        s = {(j, i): row(c[i], j) for i in range(SUB) for j in range(i + 1)}
        r = jnp.zeros(shape, jnp.float32)
        for j in range(SUB):
            at = sub == j
            pivot = s[j, j]
            inv, root = 1.0 / pivot, lax.rsqrt(pivot)
            f = jnp.where(at, -inv, c[j] * inv)
            t_j = row(t, j)
            r = jnp.where(at, t_j * root, r)
            t = jnp.where(at, 0.0, t) - f * t_j
            scaled = {i: s[j, i] * inv for i in range(j + 1, SUB)}
            for i in range(j + 1, SUB):
                c[i] = jnp.where(at, 0.0, c[i]) - f * s[j, i]
                for h in range(j + 1, i + 1):
                    s[h, i] = s[h, i] - scaled[h] * s[j, i]
        done.append(jnp.where((lane >= sub + p * SUB), r, 0.0))
        if p + 1 < tiles:
            rows = [row(t, i) for i in range(SUB)]
            later = range(p + 1, tiles)
            terms = [[col(m[q], p * SUB + i) * rows[i] for q in later] for i in range(SUB)]
            for at, q in enumerate(later):
                m[q] = m[q] - tree([terms[i][at] for i in range(SUB)])
    done = jnp.concatenate(done, axis=0)
    return done[:, :n], done[:, n:]


def factor(block, ones_ref):
    n = block.shape[0]
    if n <= BASE or n % (2 * SUB):
        return factor_base(block, ones_ref)
    h = n // 2
    r11, w11 = factor(block[:h, :h], ones_ref)
    r12 = dot(w11, block[:h, h:], ((1,), (0,)), HIGHEST)
    r21 = r12.T
    r22, w22 = factor(block[h:, h:] - dot(r21, r12, ((1,), (0,)), HIGHEST), ones_ref)
    w21 = -dot(w22, dot(r21, w11, ((1,), (0,)), HIGHEST), ((1,), (0,)), HIGHEST)
    zero = jnp.zeros((h, h), jnp.float32)
    return (
        jnp.concatenate([jnp.concatenate([r11, r12], axis=1), jnp.concatenate([zero, r22], axis=1)], axis=0),
        jnp.concatenate([jnp.concatenate([w11, zero], axis=1), jnp.concatenate([w21, w22], axis=1)], axis=0),
    )


def factor_kernel(
    gram_ref, cross_ref, sketch_hbm, r_ref, basis_hbm, proj_ref,
    inv_ref, ones_ref, sketch_ref, basis_ref, load_sem, store_sems,
):
    load = pltpu.make_async_copy(sketch_hbm, sketch_ref, load_sem)
    load.start()
    ones_ref[...] = jnp.ones_like(ones_ref)
    half = gram_ref.shape[1]
    days = cross_ref.shape[0] // 2
    r11, w11 = factor(gram_ref[0:half, :], ones_ref)
    r12 = dot(w11, gram_ref[half : 2 * half, :], ((1,), (0,)), HIGHEST)
    r21 = r12.T
    rest = gram_ref[2 * half :, :] - dot(r21, r12, ((1,), (0,)), HIGHEST)
    mixed = dot(r21, w11, ((1,), (0,)), HIGHEST)
    r22, w22 = factor(rest, ones_ref)
    w21 = -dot(w22, mixed, ((1,), (0,)), HIGHEST)
    zero = jnp.zeros((half, half), jnp.float32)
    r_ref[0:half, 0:half] = r11
    r_ref[0:half, half:] = r12
    r_ref[half:, 0:half] = zero
    r_ref[half:, half:] = r22
    inv_ref[0:half, 0:half] = w11
    inv_ref[0:half, half:] = zero
    inv_ref[half:, 0:half] = w21
    inv_ref[half:, half:] = w22
    rows = proj_ref.shape[1]
    mine = inv_ref[pl.ds(pl.multiple_of(lax.axis_index("cell") * rows, SUB), rows), :]
    proj_ref[...] = dot(cross_ref[0:days, :], mine[:, :half], ((1,), (1,)), HIGHEST) + dot(
        cross_ref[days:, :], mine[:, half:], ((1,), (1,)), HIGHEST)
    whole = inv_ref[...]
    high = whole.astype(jnp.bfloat16)
    low = (whole - high.astype(jnp.float32)).astype(jnp.bfloat16)
    load.wait()
    stores = []
    for rows in chunks_of(sketch_ref.shape[0], BASIS_STEP):
        part = sketch_ref[rows, :]
        exact = dot(part, high, ((1,), (1,))) + dot(part, low, ((1,), (1,)))
        basis_ref[rows, :] = exact.astype(jnp.bfloat16)
        stores.append(pltpu.make_async_copy(basis_ref.at[rows, :], basis_hbm.at[rows, :], store_sems.at[len(stores)]))
        stores[-1].start()
    for store in stores:
        store.wait()


def local(cells, grps, sketch, slab):
    k, days = sketch.shape[1], slab.shape[1]
    blocks, cross = reduced(sketch, slab, cells, grps)
    vmem = pl.BlockSpec(memory_space=pltpu.VMEM)
    hbm = pl.BlockSpec(memory_space=pl.ANY)
    r_factor, basis, projected = pl.pallas_call(
        factor_kernel,
        out_shape=(
            jax.ShapeDtypeStruct((k, k), jnp.float32),
            jax.ShapeDtypeStruct(sketch.shape, jnp.bfloat16),
            jax.ShapeDtypeStruct((days // grps, k // cells), jnp.float32),
        ),
        in_specs=[vmem, vmem, hbm],
        out_specs=(vmem, hbm, vmem),
        scratch_shapes=[
            pltpu.VMEM((k, k), jnp.float32),
            pltpu.VMEM((SUB, k), jnp.float32),
            pltpu.VMEM(sketch.shape, jnp.bfloat16),
            pltpu.VMEM(sketch.shape, jnp.bfloat16),
            pltpu.SemaphoreType.DMA,
            pltpu.SemaphoreType.DMA((len(chunks_of(sketch.shape[0], BASIS_STEP)),)),
        ],
        name="factor_and_basis",
    )(blocks, cross, sketch)
    return r_factor, basis, projected.T


def solution(mesh):
    cells, grps = mesh.shape["cell"], mesh.shape["grp"]
    in_specs = (P(("parts", "cell", "grp"), None), P(("parts", "cell", "grp"), None))
    out_specs = (P("parts", None), P(("parts", "cell", "grp"), None), P(("parts", "cell"), "grp"))
    return jax.shard_map(
        functools.partial(local, cells, grps), mesh=mesh, in_specs=in_specs, out_specs=out_specs, check_vma=False)
```

profile of v0, /device:TPU:0, one launch (start us, length us, event | category | flops | bytes accessed | tf_op | source)
XLA Modules:
  0.0 33.0 jit_solution(12220728211408884581)
XLA Ops:
  0.6 19.3 %reduce_sums.1 = (f32[384,128]{1,0:T(8,128)}, f32[64,128]{1,0:T(8,128)}) custom-call(bf16[3072,256]{1,0:T(8,128)(2,1)} %sketch_hbm.3, bf16[3072,128]{1,0:T(8,128)(2,1)} %slab_hbm.1), custom_call_target="tpu_custom_call" | custom-call | tf_op jit(solution)/shard_map/reduce_sums/pallas_call | solution.py:155
  20.0 13.0 %factor_and_basis.1 = (f32[256,256]{1,0:T(8,128)}, bf16[3072,256]{1,0:T(8,128)(2,1)}, f32[32,64]{1,0:T(8,128)}) custom-call(f32[384,128]{1,0:T(8,128)} %get-tuple-element.8.gram_ref, f32[64,128]{1,0:T(8,128)} %get-tuple-element.9.cross_ref, bf16[3072,256]{1,0:T(8,128)(2,1)} %sketch_hbm.3), custom_call_target="tpu_custom_call" | custom-call | tf_op jit(solution)/shard_map/factor_and_basis/pallas_call | solution.py:297
where the time goes:
time: 33.1 us; the launch traced here: 33 us
  Pallas kernels  32.3 us (98%)
  between operations  0.64 us (2%)
    pallas_call x1, Pallas kernels, reduced(): pl.pallas_call(functools.partial(reduce_kernel, cells, grps), out_shape=(...  19.3 us
    pallas_call x1, Pallas kernels, local(): pl.pallas_call(factor_kernel, out_shape=(jax.ShapeDtypeStruct((k, k), jnp...  13 us

commit v1 on v0

v1 whole, which is shorter than its diff:
```python
import functools

import jax
import jax.numpy as jnp
from jax import lax
from jax.experimental import pallas as pl
from jax.experimental.pallas import tpu as pltpu
from jax.sharding import PartitionSpec as P

SUB = 8
CORES = 2
FACTOR_VMEM = 64_500_000
BASIS_VMEM = 20 * 2**20
SUM_STEP = 768
BASIS_STEP = 512
HIGHEST = lax.Precision.HIGHEST


def dot(a, b, contract, precision=None):
    return lax.dot_general(
        a, b, (contract, ((), ())), precision=precision, preferred_element_type=jnp.float32
    )


def chunks_of(total, step):
    return [pl.ds(start, min(step, total - start)) for start in range(0, total, step)]


def sums_over(a_ref, b_ref, loads):
    total = None
    for rows, load in loads:
        load.wait()
        part = dot(a_ref[rows, :], b_ref[rows, :], ((0,), (0,)))
        total = part if total is None else total + part
    return total


def tree(terms):
    while len(terms) > 1:
        terms = [a + b for a, b in zip(terms[::2], terms[1::2])]
    return terms[0]


def factor_base(block, ones_ref):
    n = block.shape[0]
    shape = (SUB, 2 * n)
    ones = ones_ref[:, : 2 * n]
    tiles = n // SUB
    sub = lax.broadcasted_iota(jnp.int32, shape, 0)
    lane = lax.broadcasted_iota(jnp.int32, shape, 1)
    eye = jnp.where(
        lax.broadcasted_iota(jnp.int32, (n, n), 0) == lax.broadcasted_iota(jnp.int32, (n, n), 1), 1.0, 0.0)
    wide = jnp.concatenate([block, eye.astype(jnp.float32)], axis=1)
    m = [wide[q * SUB : (q + 1) * SUB, :] for q in range(tiles)]
    done = []

    def row(x, j):
        return jnp.broadcast_to(x[j : j + 1, :], shape)

    def col(x, j):
        return jnp.broadcast_to(x[:, j : j + 1], shape)

    for p in range(tiles):
        t = m[p]
        c = [col(t, p * SUB + i) * ones for i in range(SUB)]
        s = {(j, i): row(c[i], j) for i in range(SUB) for j in range(i + 1)}
        r = jnp.zeros(shape, jnp.float32)
        for j in range(SUB):
            at = sub == j
            pivot = s[j, j]
            inv, root = 1.0 / pivot, lax.rsqrt(pivot)
            f = jnp.where(at, -inv, c[j] * inv)
            t_j = row(t, j)
            r = jnp.where(at, t_j * root, r)
            t = jnp.where(at, 0.0, t) - f * t_j
            scaled = {i: s[j, i] * inv for i in range(j + 1, SUB)}
            for i in range(j + 1, SUB):
                c[i] = jnp.where(at, 0.0, c[i]) - f * s[j, i]
                for h in range(j + 1, i + 1):
                    s[h, i] = s[h, i] - scaled[h] * s[j, i]
        done.append(jnp.where((lane >= sub + p * SUB), r, 0.0))
        if p + 1 < tiles:
            rows = [row(t, i) for i in range(SUB)]
            later = range(p + 1, tiles)
            terms = [[col(m[q], p * SUB + i) * rows[i] for q in later] for i in range(SUB)]
            for at, q in enumerate(later):
                m[q] = m[q] - tree([terms[i][at] for i in range(SUB)])
    done = jnp.concatenate(done, axis=0)
    return done[:, :n], done[:, n:]


def extend(r11, w11, g12, g22, ones_ref):
    h = r11.shape[0]
    r12 = dot(w11, g12, ((1,), (0,)), HIGHEST)
    r21 = r12.T
    r22, w22 = factor_base(g22 - dot(r21, r12, ((1,), (0,)), HIGHEST), ones_ref)
    w21 = -dot(w22, dot(r21, w11, ((1,), (0,)), HIGHEST), ((1,), (0,)), HIGHEST)
    zero = jnp.zeros((h, h), jnp.float32)
    return (
        jnp.concatenate([jnp.concatenate([r11, r12], axis=1), jnp.concatenate([zero, r22], axis=1)], axis=0),
        jnp.concatenate([jnp.concatenate([w11, zero], axis=1), jnp.concatenate([w21, w22], axis=1)], axis=0),
    )


def factor_kernel(
    cells, grps, sketch_hbm, slab_hbm, r_ref, inv_ref, cross_ref, sketch_ref,
    slab_ref, sketch_sems, slab_sems, ones_ref,
    own_a, core_a, chip_a, all_a, own_b, core_b, chip_b, all_b,
    own_c, grp_c, cell_c, all_c, own_x, grp_x, cell_x,
    core_send, core_recv, a_send, a_recv, b_send, b_recv, gc_send, gc_recv, zc_send, zc_recv,
    ac_send, ac_recv, gx_send, gx_recv, zx_send, zx_recv,
):
    def loading(source, target, sems):
        loads = []
        for i, rows in enumerate(chunks_of(source.shape[0], SUM_STEP)):
            load = pltpu.make_async_copy(source.at[rows, :], target.at[rows, :], sems.at[i])
            load.start()
            loads.append((rows, load))
        return loads

    sketch_loads = loading(sketch_hbm, sketch_ref, sketch_sems)
    slab_loads = loading(slab_hbm, slab_ref, slab_sems)
    me_c = lax.axis_index("cell")
    me_g = lax.axis_index("grp")
    chips_x = grps // CORES
    me_x, core = lax.div(me_g, CORES), lax.rem(me_g, CORES)
    me_chip = me_c * chips_x + me_x
    other = me_x * CORES + (1 - core)
    half = own_b.shape[1]
    quarter = half // 2
    started = []

    def send(source, target, send_sem, recv_sem, device):
        copy = pltpu.make_async_remote_copy(
            src_ref=source, dst_ref=target, send_sem=send_sem, recv_sem=recv_sem,
            device_id=device, device_id_type=pl.DeviceIdType.MESH)
        copy.start()
        started.append(copy)
        return copy

    def rows_of(ref, index, count):
        return ref.at[pl.ds(pl.multiple_of(index * count, SUB), count), :]

    grp_peers = [{"grp": lax.rem(me_g + d, grps)} for d in range(1, grps)]
    cell_peers = [{"cell": lax.rem(me_c + d, cells)} for d in range(1, cells)]
    chip_peers = [
        {"cell": lax.rem(me_c + dc, cells), "grp": lax.rem(me_x + dx, chips_x) * CORES + core}
        for dx in reversed(range(chips_x)) for dc in sorted(range(cells), key=lambda d: -min(d, cells - d)) if dc or dx]

    barrier = pltpu.get_barrier_semaphore()
    beyond = [{"cell": peer["cell"], "grp": peer["grp"]} for peer in chip_peers]
    for peer in beyond + [p for d, p in enumerate(grp_peers, 1)]:
        pl.semaphore_signal(barrier, inc=1, device_id=peer, device_id_type=pl.DeviceIdType.MESH)

    gram = sums_over(sketch_ref, sketch_ref, sketch_loads)
    eighth = quarter // 2
    own_a[...] = jnp.concatenate([gram[:eighth, :quarter], gram[eighth:quarter, :quarter]], axis=1)
    own_b[...] = jnp.concatenate([gram[:quarter, quarter:half], gram[quarter:half, quarter:half]], axis=1)
    pl.semaphore_wait(barrier, len(beyond) + len(grp_peers))

    def halves(own, landing, index):
        count = own.shape[0] // CORES
        return send(rows_of(own, 1 - core, count), landing, core_send.at[index], core_recv.at[index], {"grp": other})

    a1 = halves(own_a, core_a, 0)
    b1 = halves(own_b, core_b, 1)
    own_c[0:half, :] = gram[:half, half:]
    own_c[half:, :] = gram[half:, half:]

    def to_grps(own, landing, send_sems, recv_sems):
        count = own.shape[0] // grps
        return [
            send(rows_of(own, peer["grp"], count), landing.at[i], send_sems.at[i], recv_sems.at[i], peer)
            for i, peer in enumerate(grp_peers)]

    def sum_grps(copies, own, landing, slots):
        count = own.shape[0] // grps
        for copy in copies:
            copy.wait_recv()
        slots[me_c] = tree([own[pl.ds(pl.multiple_of(me_g * count, SUB), count), :]] + [landing[i] for i in range(grps - 1)])

    def spread(slots, me, peers, send_sems, recv_sems):
        return [send(slots.at[me], slots.at[me], send_sems.at[i], recv_sems.at[i], peer) for i, peer in enumerate(peers)]

    def sum_slots(copies, slots):
        for copy in copies:
            copy.wait_recv()
        return tree([slots[i] for i in range(slots.shape[0])])

    c1 = to_grps(own_c, grp_c, gc_send, gc_recv)

    def chip_sum(copy, own, landing, slots, send_sems, recv_sems):
        count = own.shape[0] // CORES
        copy.wait_recv()
        slots[me_chip] = own[pl.ds(pl.multiple_of(core * count, SUB), count), :] + landing[...]
        return spread(slots, me_chip, chip_peers, send_sems, recv_sems)

    a2 = chip_sum(a1, own_a, core_a, chip_a, a_send, a_recv)
    b2 = chip_sum(b1, own_b, core_b, chip_b, b_send, b_recv)

    cross = sums_over(slab_ref, sketch_ref, slab_loads)
    days = cross.shape[0] // grps
    for g in range(grps):
        own_x[2 * g * days : (2 * g + 1) * days, :] = cross[g * days : (g + 1) * days, :half]
        own_x[(2 * g + 1) * days : 2 * (g + 1) * days, :] = cross[g * days : (g + 1) * days, half:]

    sum_grps(c1, own_c, grp_c, cell_c)
    c2 = spread(cell_c, me_c, cell_peers, zc_send, zc_recv)

    def both(copies, slots, target, index):
        target[core] = sum_slots(copies, slots)
        return send(target.at[core], target.at[core], core_send.at[index], core_recv.at[index], {"grp": other})

    a3 = both(a2, chip_a, all_a, 2)
    b3 = both(b2, chip_b, all_b, 3)
    x1 = to_grps(own_x, grp_x, gx_send, gx_recv)
    ones_ref[...] = jnp.ones_like(ones_ref)

    a3.wait_recv()
    packed = jnp.concatenate([all_a[i] for i in range(CORES)], axis=0)
    first = jnp.concatenate([packed[:, :quarter], packed[:, quarter:]], axis=0)
    r_00, w_00 = factor_base(first, ones_ref)

    count = own_c.shape[0] // grps
    all_c[pl.ds(pl.multiple_of(me_g * count, SUB), count), :] = sum_slots(c2, cell_c)
    c3 = [
        send(rows_of(all_c, me_g, count), rows_of(all_c, me_g, count), ac_send.at[i], ac_recv.at[i], peer)
        for i, peer in enumerate(grp_peers)]

    b3.wait_recv()
    packed = jnp.concatenate([all_b[i] for i in range(CORES)], axis=0)
    r11, w11 = extend(r_00, w_00, packed[:, :quarter], packed[:, quarter:], ones_ref)
    zero = jnp.zeros((half, half), jnp.float32)
    r_ref[0:half, 0:half] = r11
    r_ref[half:, 0:half] = zero
    inv_ref[0:half, 0:half] = w11
    inv_ref[0:half, half:] = zero

    sum_grps(x1, own_x, grp_x, cell_x)
    x2 = spread(cell_x, me_c, cell_peers, zx_send, zx_recv)

    for copy in c3:
        copy.wait_recv()
    r12 = dot(w11, all_c[0:half, :], ((1,), (0,)), HIGHEST)
    r21 = r12.T
    rest = all_c[half:, :] - dot(r21, r12, ((1,), (0,)), HIGHEST)
    mixed = dot(r21, w11, ((1,), (0,)), HIGHEST)
    r_ref[0:half, half:] = r12
    r_00, w_00 = factor_base(rest[:quarter, :quarter], ones_ref)
    r22, w22 = extend(r_00, w_00, rest[:quarter, quarter:], rest[quarter:, quarter:], ones_ref)
    r_ref[half:, half:] = r22
    inv_ref[half:, 0:half] = -dot(w22, mixed, ((1,), (0,)), HIGHEST)
    inv_ref[half:, half:] = w22
    cross_ref[...] = sum_slots(x2, cell_x)
    for copy in started:
        copy.wait_send()


def factored(sketch, slab, cells, grps):
    k, days = sketch.shape[1], slab.shape[1]
    half, quarter = k // 2, k // 4
    chips = cells * grps // CORES
    f32 = jnp.float32
    dma = pltpu.SemaphoreType.DMA
    a_rows, b_rows, c_rows, x_rows = quarter // 2, quarter, 2 * half, 2 * days
    assert grps % CORES == 0 and cells > 1 and k % (8 * SUB) == 0
    assert c_rows % (SUB * grps) == 0 and x_rows % (2 * SUB * grps) == 0

    def small(rows):
        part = rows // CORES
        return [pltpu.VMEM((rows, half), f32), pltpu.VMEM((part, half), f32),
                pltpu.VMEM((chips, part, half), f32), pltpu.VMEM((CORES, part, half), f32)]

    def large(rows):
        part = rows // grps
        return [pltpu.VMEM((rows, half), f32), pltpu.VMEM((grps - 1, part, half), f32),
                pltpu.VMEM((cells, part, half), f32)]

    return pl.pallas_call(
        functools.partial(factor_kernel, cells, grps),
        out_shape=(
            jax.ShapeDtypeStruct((k, k), f32),
            jax.ShapeDtypeStruct((k, k), f32),
            jax.ShapeDtypeStruct((x_rows // grps, half), f32),
            jax.ShapeDtypeStruct(sketch.shape, sketch.dtype),
        ),
        in_specs=[pl.BlockSpec(memory_space=pltpu.HBM)] * 2,
        out_specs=(pl.BlockSpec(memory_space=pltpu.VMEM),) * 4,
        scratch_shapes=[
            pltpu.VMEM(slab.shape, slab.dtype),
            dma((len(chunks_of(sketch.shape[0], SUM_STEP)),)),
            dma((len(chunks_of(slab.shape[0], SUM_STEP)),)),
            pltpu.VMEM((SUB, k), f32),
        ] + small(a_rows) + small(b_rows) + large(c_rows) + [pltpu.VMEM((c_rows, half), f32)] + large(x_rows)
        + [dma((4,))] * 2 + [dma((chips - 1,))] * 4
        + [dma((grps - 1,))] * 2 + [dma((cells - 1,))] * 2 + [dma((grps - 1,))] * 4 + [dma((cells - 1,))] * 2,
        compiler_params=pltpu.CompilerParams(collective_id=0, has_side_effects=True, vmem_limit_bytes=FACTOR_VMEM),
        name="reduce_and_factor",
    )(sketch, slab)


def basis_kernel(
    r_in, inv_ref, cross_ref, sketch_ref, r_out, basis_hbm, proj_ref, basis_ref, store_sems,
):
    steps = chunks_of(sketch_ref.shape[0], BASIS_STEP)
    half = cross_ref.shape[1]
    days = cross_ref.shape[0] // 2
    r_out[...] = r_in[...]
    whole = inv_ref[...]
    high = whole.astype(jnp.bfloat16)
    low = (whole - high.astype(jnp.float32)).astype(jnp.bfloat16)
    stores = []
    for i, rows in enumerate(steps):
        part = sketch_ref[rows, :]
        exact = dot(part, high, ((1,), (1,))) + dot(part, low, ((1,), (1,)))
        basis_ref[rows, :] = exact.astype(jnp.bfloat16)
        stores.append(pltpu.make_async_copy(basis_ref.at[rows, :], basis_hbm.at[rows, :], store_sems.at[i]))
        stores[-1].start()
    count = proj_ref.shape[1]
    mine = inv_ref[pl.ds(pl.multiple_of(lax.axis_index("cell") * count, SUB), count), :]
    proj_ref[...] = dot(cross_ref[0:days, :], mine[:, :half], ((1,), (1,)), HIGHEST) + dot(
        cross_ref[days:, :], mine[:, half:], ((1,), (1,)), HIGHEST)
    for store in stores:
        store.wait()


def local(cells, grps, sketch, slab):
    k, days = sketch.shape[1], slab.shape[1]
    r_in, inverse, cross, held = factored(sketch, slab, cells, grps)
    vmem = pl.BlockSpec(memory_space=pltpu.VMEM)
    hbm = pl.BlockSpec(memory_space=pl.ANY)
    steps = len(chunks_of(sketch.shape[0], BASIS_STEP))
    r_factor, basis, projected = pl.pallas_call(
        basis_kernel,
        out_shape=(
            jax.ShapeDtypeStruct((k, k), jnp.float32),
            jax.ShapeDtypeStruct(sketch.shape, jnp.bfloat16),
            jax.ShapeDtypeStruct((days // grps, k // cells), jnp.float32),
        ),
        in_specs=[vmem] * 4,
        out_specs=(vmem, hbm, vmem),
        scratch_shapes=[
            pltpu.VMEM(sketch.shape, jnp.bfloat16),
            pltpu.SemaphoreType.DMA((steps,)),
        ],
        compiler_params=pltpu.CompilerParams(vmem_limit_bytes=BASIS_VMEM),
        name="basis",
    )(r_in, inverse, cross, held)
    return r_factor, basis, projected.T


def solution(mesh):
    cells, grps = mesh.shape["cell"], mesh.shape["grp"]
    in_specs = (P(("parts", "cell", "grp"), None), P(("parts", "cell", "grp"), None))
    out_specs = (P("parts", None), P(("parts", "cell", "grp"), None), P(("parts", "cell"), "grp"))
    return jax.shard_map(
        functools.partial(local, cells, grps), mesh=mesh, in_specs=in_specs, out_specs=out_specs, check_vma=False)
```

time: 33.1 us -> 32.9 us (level)
  Pallas kernels: 32.3 us -> 27.9 us
  local copies, waits for them, and re-layouts: 0 us -> 4.06 us
    pallas_call x2, Pallas kernels: 32.3 us -> 27.9 us  [the longest x1 25.3 us: factored(): pl.pallas_call(functools.partial(factor_kernel, cells, grps), out_shape=(...]
    unnamed x0 -> x8, local copies, waits for them, and re-layouts: none -> 4.06 us
where the time goes in v1:
time: 32.9 us; the launch traced here: 32.6 us
  Pallas kernels  27.9 us (85%)
  local copies, waits for them, and re-layouts  4.06 us (12%)
  between operations  0.65 us (2%)
    pallas_call x1, Pallas kernels, factored(): pl.pallas_call(functools.partial(factor_kernel, cells, grps), out_shape=(...  25.3 us
    unnamed x8, local copies, waits for them, and re-layouts  4.06 us
    pallas_call x1, Pallas kernels, local(): pl.pallas_call(basis_kernel, out_shape=(jax.ShapeDtypeStruct((k, k), jnp....  2.63 us

profile of v1, /device:TPU:0, one launch (start us, length us, event | category | flops | bytes accessed | tf_op | source)
XLA Modules:
  0.0 32.6 jit_solution(14376707856725574020)
XLA Ops:
  0.6 25.3 %reduce_and_factor.1 = (f32[256,256]{1,0:T(8,128)}, f32[256,256]{1,0:T(8,128)}, f32[64,128]{1,0:T(8,128)}, bf16[3072,256]{1,0:T(8,128)(2,1)}) custom-call(bf16[3072,256]{1,0:T(8,128)(2,1)} %sketch_hbm.1, bf16[3072,128]{1,0:T(8,128)(2,1)} %slab_hbm.1), custom_call_target="tpu_custom_call" | custom-call | tf_op jit(solution)/shard_map/reduce_and_factor/pallas_call | solution.py:279
  25.9 0.0 copy-start
  25.9 1.4 %copy-done = bf16[3072,256]{1,0:T(8,128)(2,1)S(1)} copy-done((bf16[3072,256]{1,0:T(8,128)(2,1)S(1)}, bf16[3072,256]{1,0:T(8,128)(2,1)}, u32[]{:S(2)}) %copy-start) | copy-done | bytes 1572888
  27.3 0.0 copy-start.1
  27.3 0.9 %copy-done.1 = f32[256,256]{1,0:T(8,128)S(1)} copy-done((f32[256,256]{1,0:T(8,128)S(1)}, f32[256,256]{1,0:T(8,128)}, u32[]{:S(2)}) %copy-start.1) | copy-done | bytes 262168
  28.3 0.0 copy-start.2
  28.3 0.9 %copy-done.2 = f32[256,256]{1,0:T(8,128)S(1)} copy-done((f32[256,256]{1,0:T(8,128)S(1)}, f32[256,256]{1,0:T(8,128)}, u32[]{:S(2)}) %copy-start.2) | copy-done | bytes 262168
  29.2 0.0 copy-start.3
  29.2 0.8 %copy-done.3 = f32[64,128]{1,0:T(8,128)S(1)} copy-done((f32[64,128]{1,0:T(8,128)S(1)}, f32[64,128]{1,0:T(8,128)}, u32[]{:S(2)}) %copy-start.3) | copy-done | bytes 32792
  30.0 2.6 %basis.1 = (f32[256,256]{1,0:T(8,128)}, bf16[3072,256]{1,0:T(8,128)(2,1)}, f32[32,64]{1,0:T(8,128)}) custom-call(f32[256,256]{1,0:T(8,128)S(1)} %copy-done.1, f32[256,256]{1,0:T(8,128)S(1)} %copy-done.2, f32[64,128]{1,0:T(8,128)S(1)} %copy-done.3, bf16[3072,256]{1,0:T(8,128)(2,1)S(1)} %copy-done), custom_call_target="tpu_custom_call" | custom-call | tf_op jit(solution)/shard_map/basis/pallas_call | solution.py:333
Async XLA Ops:
  25.9 1.4 %copy-start = (bf16[3072,256]{1,0:T(8,128)(2,1)S(1)}, bf16[3072,256]{1,0:T(8,128)(2,1)}, u32[]{:S(2)}) copy-start(bf16[3072,256]{1,0:T(8,128)(2,1)} %get-tuple-element.13.sketch_ref) | copy-start | bytes 4718596
  27.3 0.9 %copy-start.1 = (f32[256,256]{1,0:T(8,128)S(1)}, f32[256,256]{1,0:T(8,128)}, u32[]{:S(2)}) copy-start(f32[256,256]{1,0:T(8,128)} %get-tuple-element.10.r_in) | copy-start | bytes 786436
  28.3 0.9 %copy-start.2 = (f32[256,256]{1,0:T(8,128)S(1)}, f32[256,256]{1,0:T(8,128)}, u32[]{:S(2)}) copy-start(f32[256,256]{1,0:T(8,128)} %get-tuple-element.11.inv_ref) | copy-start | bytes 786436
  29.2 0.8 %copy-start.3 = (f32[64,128]{1,0:T(8,128)S(1)}, f32[64,128]{1,0:T(8,128)}, u32[]{:S(2)}) copy-start(f32[64,128]{1,0:T(8,128)} %get-tuple-element.12.cross_ref) | copy-start | bytes 98308

commit v2 on v1

--- a/solution.py
+++ b/solution.py
@@ -9,8 +9,7 @@
 
 SUB = 8
 CORES = 2
-FACTOR_VMEM = 64_500_000
-BASIS_VMEM = 20 * 2**20
+VMEM_LIMIT = 20 * 2**20
 SUM_STEP = 768
 BASIS_STEP = 512
 HIGHEST = lax.Precision.HIGHEST
@@ -294,9 +293,9 @@
         ] + small(a_rows) + small(b_rows) + large(c_rows) + [pltpu.VMEM((c_rows, half), f32)] + large(x_rows)
         + [dma((4,))] * 2 + [dma((chips - 1,))] * 4
         + [dma((grps - 1,))] * 2 + [dma((cells - 1,))] * 2 + [dma((grps - 1,))] * 4 + [dma((cells - 1,))] * 2,
-        compiler_params=pltpu.CompilerParams(collective_id=0, has_side_effects=True, vmem_limit_bytes=FACTOR_VMEM),
+        compiler_params=pltpu.CompilerParams(collective_id=0, has_side_effects=True, vmem_limit_bytes=VMEM_LIMIT),
         name="reduce_and_factor",
-    )(sketch, slab)
+    )(pltpu.with_memory_space_constraint(sketch, pltpu.HBM), pltpu.with_memory_space_constraint(slab, pltpu.HBM))
 
 
 def basis_kernel(
@@ -343,7 +342,7 @@
             pltpu.VMEM(sketch.shape, jnp.bfloat16),
             pltpu.SemaphoreType.DMA((steps,)),
         ],
-        compiler_params=pltpu.CompilerParams(vmem_limit_bytes=BASIS_VMEM),
+        compiler_params=pltpu.CompilerParams(vmem_limit_bytes=VMEM_LIMIT),
         name="basis",
     )(r_in, inverse, cross, held)
     return r_factor, basis, projected.T

time: 32.9 us -> 27.3 us (0.83)
  local copies, waits for them, and re-layouts: 4.06 us -> 0 us
  Pallas kernels: 27.9 us -> 26.6 us
    unnamed x8 -> x0, local copies, waits for them, and re-layouts: 4.06 us -> none
    pallas_call x1, Pallas kernels: 25.3 us -> 23.9 us  [factored(): pl.pallas_call(functools.partial(factor_kernel, cells, grps), out_shape=(...]
where the time goes in v2:
time: 27.3 us; the launch traced here: 27.2 us
  Pallas kernels  26.6 us (97%)
  between operations  0.64 us (2%)
    pallas_call x1, Pallas kernels, factored(): pl.pallas_call(functools.partial(factor_kernel, cells, grps), out_shape=(...  23.9 us
    pallas_call x1, Pallas kernels, local(): pl.pallas_call(basis_kernel, out_shape=(jax.ShapeDtypeStruct((k, k), jnp....  2.64 us

profile of v2, /device:TPU:0, one launch (start us, length us, event | category | flops | bytes accessed | tf_op | source)
XLA Modules:
  0.0 27.2 jit_solution(4346655223135776581)
XLA Ops:
  0.6 23.9 %reduce_and_factor.1 = (f32[256,256]{1,0:T(8,128)S(1)}, f32[256,256]{1,0:T(8,128)S(1)}, f32[64,128]{1,0:T(8,128)S(1)}, bf16[3072,256]{1,0:T(8,128)(2,1)S(1)}) custom-call(bf16[3072,256]{1,0:T(8,128)(2,1)} %sketch_hbm.1, bf16[3072,128]{1,0:T(8,128)(2,1)} %slab_hbm.1), custom_call_target="tpu_custom_call" | custom-call | tf_op jit(solution)/shard_map/reduce_and_factor/pallas_call | solution.py:278
  24.6 2.6 %basis.1 = (f32[256,256]{1,0:T(8,128)}, bf16[3072,256]{1,0:T(8,128)(2,1)}, f32[32,64]{1,0:T(8,128)}) custom-call(f32[256,256]{1,0:T(8,128)S(1)} %get-tuple-element.10.r_in, f32[256,256]{1,0:T(8,128)S(1)} %get-tuple-element.11.inv_ref, f32[64,128]{1,0:T(8,128)S(1)} %get-tuple-element.12.cross_ref, bf16[3072,256]{1,0:T(8,128)(2,1)S(1)} %get-tuple-element.13.sketch_ref), custom_call_target="tpu_custom_call" | custom-call | tf_op jit(solution)/shard_map/basis/pallas_call | solution.py:332

commit v3 on v2

--- a/solution.py
+++ b/solution.py
@@ -104,9 +104,9 @@
 def factor_kernel(
     cells, grps, sketch_hbm, slab_hbm, r_ref, inv_ref, cross_ref, sketch_ref,
     slab_ref, sketch_sems, slab_sems, ones_ref,
-    own_a, core_a, chip_a, all_a, own_b, core_b, chip_b, all_b,
+    own_a, core_a, chip_a, all_a, own_b, grp_b, cell_b, all_b,
     own_c, grp_c, cell_c, all_c, own_x, grp_x, cell_x,
-    core_send, core_recv, a_send, a_recv, b_send, b_recv, gc_send, gc_recv, zc_send, zc_recv,
+    core_send, core_recv, a_send, a_recv, gb_send, gb_recv, zb_send, zb_recv, gc_send, gc_recv, zc_send, zc_recv,
     ac_send, ac_recv, gx_send, gx_recv, zx_send, zx_recv,
 ):
     def loading(source, target, sems):
@@ -162,9 +162,17 @@
         return send(rows_of(own, 1 - core, count), landing, core_send.at[index], core_recv.at[index], {"grp": other})
 
     a1 = halves(own_a, core_a, 0)
-    b1 = halves(own_b, core_b, 1)
+    count = own_b.shape[0] // CORES
+    b1 = [
+        send(rows_of(own_b, lax.rem(peer["grp"], CORES), count), grp_b.at[me_g], gb_send.at[i], gb_recv.at[i], peer)
+        for i, peer in enumerate(grp_peers)]
     own_c[0:half, :] = gram[:half, half:]
-    own_c[half:, :] = gram[half:, half:]
+    own_c[half : half + quarter, :] = gram[half : half + quarter, half:]
+    last = gram[half + quarter :, half + quarter :]
+    own_c[half + quarter : half + quarter + eighth, :] = jnp.concatenate([last[:eighth], last[eighth:]], axis=1)
+    spare = own_c.shape[0] - half - quarter - eighth
+    if spare:
+        own_c[half + quarter + eighth :, :] = jnp.zeros((spare, half), jnp.float32)
 
     def to_grps(own, landing, send_sems, recv_sems):
         count = own.shape[0] // grps
@@ -195,7 +203,6 @@
         return spread(slots, me_chip, chip_peers, send_sems, recv_sems)
 
     a2 = chip_sum(a1, own_a, core_a, chip_a, a_send, a_recv)
-    b2 = chip_sum(b1, own_b, core_b, chip_b, b_send, b_recv)
 
     cross = sums_over(slab_ref, sketch_ref, slab_loads)
     days = cross.shape[0] // grps
@@ -203,6 +210,9 @@
         own_x[2 * g * days : (2 * g + 1) * days, :] = cross[g * days : (g + 1) * days, :half]
         own_x[(2 * g + 1) * days : 2 * (g + 1) * days, :] = cross[g * days : (g + 1) * days, half:]
 
+    grp_b[me_g] = own_b[pl.ds(pl.multiple_of(core * (own_b.shape[0] // CORES), SUB), own_b.shape[0] // CORES), :]
+    cell_b[me_c] = sum_slots(b1, grp_b)
+    b2 = spread(cell_b, me_c, cell_peers, zb_send, zb_recv)
     sum_grps(c1, own_c, grp_c, cell_c)
     c2 = spread(cell_c, me_c, cell_peers, zc_send, zc_recv)
 
@@ -211,9 +221,9 @@
         return send(target.at[core], target.at[core], core_send.at[index], core_recv.at[index], {"grp": other})
 
     a3 = both(a2, chip_a, all_a, 2)
-    b3 = both(b2, chip_b, all_b, 3)
+    ones_ref[...] = jnp.ones_like(ones_ref)
+    b3 = both(b2, cell_b, all_b, 3)
     x1 = to_grps(own_x, grp_x, gx_send, gx_recv)
-    ones_ref[...] = jnp.ones_like(ones_ref)
 
     a3.wait_recv()
     packed = jnp.concatenate([all_a[i] for i in range(CORES)], axis=0)
@@ -242,11 +252,14 @@
         copy.wait_recv()
     r12 = dot(w11, all_c[0:half, :], ((1,), (0,)), HIGHEST)
     r21 = r12.T
-    rest = all_c[half:, :] - dot(r21, r12, ((1,), (0,)), HIGHEST)
+    taken = dot(r21, r12, ((1,), (0,)), HIGHEST)
+    upper = all_c[half : half + quarter, :] - taken[:quarter]
+    last = all_c[half + quarter : half + quarter + eighth, :]
+    last = jnp.concatenate([last[:, :quarter], last[:, quarter:]], axis=0) - taken[quarter:, quarter:]
     mixed = dot(r21, w11, ((1,), (0,)), HIGHEST)
     r_ref[0:half, half:] = r12
-    r_00, w_00 = factor_base(rest[:quarter, :quarter], ones_ref)
-    r22, w22 = extend(r_00, w_00, rest[:quarter, quarter:], rest[quarter:, quarter:], ones_ref)
+    r_00, w_00 = factor_base(upper[:, :quarter], ones_ref)
+    r22, w22 = extend(r_00, w_00, upper[:, quarter:], last, ones_ref)
     r_ref[half:, half:] = r22
     inv_ref[half:, 0:half] = -dot(w22, mixed, ((1,), (0,)), HIGHEST)
     inv_ref[half:, half:] = w22
@@ -261,9 +274,10 @@
     chips = cells * grps // CORES
     f32 = jnp.float32
     dma = pltpu.SemaphoreType.DMA
-    a_rows, b_rows, c_rows, x_rows = quarter // 2, quarter, 2 * half, 2 * days
+    a_rows, b_rows, x_rows = quarter // 2, quarter, 2 * days
+    c_rows = pl.cdiv(half + quarter + quarter // 2, SUB * grps) * SUB * grps
     assert grps % CORES == 0 and cells > 1 and k % (8 * SUB) == 0
-    assert c_rows % (SUB * grps) == 0 and x_rows % (2 * SUB * grps) == 0
+    assert x_rows % (2 * SUB * grps) == 0
 
     def small(rows):
         part = rows // CORES
@@ -290,8 +304,13 @@
             dma((len(chunks_of(sketch.shape[0], SUM_STEP)),)),
             dma((len(chunks_of(slab.shape[0], SUM_STEP)),)),
             pltpu.VMEM((SUB, k), f32),
-        ] + small(a_rows) + small(b_rows) + large(c_rows) + [pltpu.VMEM((c_rows, half), f32)] + large(x_rows)
-        + [dma((4,))] * 2 + [dma((chips - 1,))] * 4
+        ] + small(a_rows) + [
+            pltpu.VMEM((b_rows, half), f32),
+            pltpu.VMEM((grps, b_rows // CORES, half), f32),
+            pltpu.VMEM((cells, b_rows // CORES, half), f32),
+            pltpu.VMEM((CORES, b_rows // CORES, half), f32),
+        ] + large(c_rows) + [pltpu.VMEM((c_rows, half), f32)] + large(x_rows)
+        + [dma((4,))] * 2 + [dma((chips - 1,))] * 2 + [dma((grps - 1,))] * 2 + [dma((cells - 1,))] * 2
         + [dma((grps - 1,))] * 2 + [dma((cells - 1,))] * 2 + [dma((grps - 1,))] * 4 + [dma((cells - 1,))] * 2,
         compiler_params=pltpu.CompilerParams(collective_id=0, has_side_effects=True, vmem_limit_bytes=VMEM_LIMIT),
         name="reduce_and_factor",

time: 27.3 us -> 26 us (0.952)
  Pallas kernels: 26.6 us -> 25.2 us
    pallas_call x1, Pallas kernels: 23.9 us -> 22.6 us  [factored(): pl.pallas_call(functools.partial(factor_kernel, cells, grps), out_shape=(...]
where the time goes in v3:
time: 26 us; the launch traced here: 25.8 us
  Pallas kernels  25.2 us (97%)
  between operations  0.64 us (2%)
    pallas_call x1, Pallas kernels, factored(): pl.pallas_call(functools.partial(factor_kernel, cells, grps), out_shape=(...  22.6 us
    pallas_call x1, Pallas kernels, local(): pl.pallas_call(basis_kernel, out_shape=(jax.ShapeDtypeStruct((k, k), jnp....  2.63 us

profile of v3, /device:TPU:0, one launch (start us, length us, event | category | flops | bytes accessed | tf_op | source)
XLA Modules:
  0.0 25.8 jit_solution(7674681968225019562)
XLA Ops:
  0.6 22.6 %reduce_and_factor.1 = (f32[256,256]{1,0:T(8,128)S(1)}, f32[256,256]{1,0:T(8,128)S(1)}, f32[64,128]{1,0:T(8,128)S(1)}, bf16[3072,256]{1,0:T(8,128)(2,1)S(1)}) custom-call(bf16[3072,256]{1,0:T(8,128)(2,1)} %sketch_hbm.1, bf16[3072,128]{1,0:T(8,128)(2,1)} %slab_hbm.1), custom_call_target="tpu_custom_call" | custom-call | tf_op jit(solution)/shard_map/reduce_and_factor/pallas_call | solution.py:292
  23.2 2.6 %basis.1 = (f32[256,256]{1,0:T(8,128)}, bf16[3072,256]{1,0:T(8,128)(2,1)}, f32[32,64]{1,0:T(8,128)}) custom-call(f32[256,256]{1,0:T(8,128)S(1)} %get-tuple-element.10.r_in, f32[256,256]{1,0:T(8,128)S(1)} %get-tuple-element.11.inv_ref, f32[64,128]{1,0:T(8,128)S(1)} %get-tuple-element.12.cross_ref, bf16[3072,256]{1,0:T(8,128)(2,1)S(1)} %get-tuple-element.13.sketch_ref), custom_call_target="tpu_custom_call" | custom-call | tf_op jit(solution)/shard_map/basis/pallas_call | solution.py:351

commit v4 on v3

--- a/solution.py
+++ b/solution.py
@@ -35,10 +35,10 @@
 
 
 def tree(terms):
+    terms=list(terms)
     while len(terms) > 1:
-        terms = [a + b for a, b in zip(terms[::2], terms[1::2])]
+        terms = [a + b for a, b in zip(terms[::2], terms[1::2])] + terms[len(terms) // 2 * 2 :]
     return terms[0]
-
 
 def factor_base(block, ones_ref):
     n = block.shape[0]
@@ -62,21 +62,30 @@
     for p in range(tiles):
         t = m[p]
         c = [col(t, p * SUB + i) * ones for i in range(SUB)]
-        s = {(j, i): row(c[i], j) for i in range(SUB) for j in range(i + 1)}
+        corner = [row(c[0], 0), row(c[1], 0), row(c[1], 1)]
         r = jnp.zeros(shape, jnp.float32)
-        for j in range(SUB):
-            at = sub == j
-            pivot = s[j, j]
-            inv, root = 1.0 / pivot, lax.rsqrt(pivot)
-            f = jnp.where(at, -inv, c[j] * inv)
-            t_j = row(t, j)
-            r = jnp.where(at, t_j * root, r)
-            t = jnp.where(at, 0.0, t) - f * t_j
-            scaled = {i: s[j, i] * inv for i in range(j + 1, SUB)}
-            for i in range(j + 1, SUB):
-                c[i] = jnp.where(at, 0.0, c[i]) - f * s[j, i]
-                for h in range(j + 1, i + 1):
-                    s[h, i] = s[h, i] - scaled[h] * s[j, i]
+        for j in range(0, SUB, 2):
+            k = j + 1
+            at_j, at_k = sub == j, sub == k
+            pair = at_j | at_k
+            a, b, d = corner
+            det = a * d - b * b
+            inv = 1.0 / det
+            root_a, root = lax.rsqrt(a), lax.rsqrt(det)
+            f_j = jnp.where(at_j, -d, jnp.where(at_k, b, c[j] * d - c[k] * b))
+            f_k = jnp.where(at_j, b, jnp.where(at_k, -a, c[k] * a - c[j] * b))
+            t_j, t_k = row(t, j), row(t, k)
+            r = jnp.where(at_j, t_j * root_a, jnp.where(at_k, (t_k * a - t_j * b) * (root_a * root), r))
+            t = jnp.where(pair, 0.0, t) - (f_j * t_j + f_k * t_k) * inv
+            if k + 1 < SUB:
+                s_j = {i: row(c[i], j) for i in range(k + 1, SUB)}
+                s_k = {i: row(c[i], k) for i in range(k + 1, SUB)}
+                e, g = k + 1, k + 2
+                v = {h: (s_j[h] * d - s_k[h] * b, s_k[h] * a - s_j[h] * b) for h in (e, g)}
+                corner = [
+                    row(c[i], h) - (v[h][0] * s_j[i] + v[h][1] * s_k[i]) * inv for h, i in ((e, e), (e, g), (g, g))]
+                for i in range(k + 1, SUB):
+                    c[i] = jnp.where(pair, 0.0, c[i]) - (f_j * s_j[i] + f_k * s_k[i]) * inv
         done.append(jnp.where((lane >= sub + p * SUB), r, 0.0))
         if p + 1 < tiles:
             rows = [row(t, i) for i in range(SUB)]
@@ -86,6 +95,15 @@
                 m[q] = m[q] - tree([terms[i][at] for i in range(SUB)])
     done = jnp.concatenate(done, axis=0)
     return done[:, :n], done[:, n:]
+
+
+def scales(block):
+    n = block.shape[0]
+    eye = lax.broadcasted_iota(jnp.int32, (n, n), 0) == lax.broadcasted_iota(jnp.int32, (n, n), 1)
+    kept = jnp.where(eye, block, 0.0)
+    across = jnp.sum(kept, axis=0, keepdims=True)
+    row, col = lax.rsqrt(across), lax.rsqrt(jnp.sum(kept, axis=1, keepdims=True))
+    return row, col, across * row
 
 
 def extend(r11, w11, g12, g22, ones_ref):
@@ -228,7 +246,8 @@
     a3.wait_recv()
     packed = jnp.concatenate([all_a[i] for i in range(CORES)], axis=0)
     first = jnp.concatenate([packed[:, :quarter], packed[:, quarter:]], axis=0)
-    r_00, w_00 = factor_base(first, ones_ref)
+    row0, col0, back0 = scales(first)
+    r_00, w_00 = factor_base(first * col0 * row0, ones_ref)
 
     count = own_c.shape[0] // grps
     all_c[pl.ds(pl.multiple_of(me_g * count, SUB), count), :] = sum_slots(c2, cell_c)
@@ -238,11 +257,14 @@
 
     b3.wait_recv()
     packed = jnp.concatenate([all_b[i] for i in range(CORES)], axis=0)
-    r11, w11 = extend(r_00, w_00, packed[:, :quarter], packed[:, quarter:], ones_ref)
+    row1, col1, back1 = scales(packed[:, quarter:])
+    r11, w11 = extend(
+        r_00, w_00, packed[:, :quarter] * col0 * row1, packed[:, quarter:] * col1 * row1, ones_ref)
+    left_row, left_col = jnp.concatenate([row0, row1], axis=1), jnp.concatenate([col0, col1], axis=0)
     zero = jnp.zeros((half, half), jnp.float32)
-    r_ref[0:half, 0:half] = r11
+    r_ref[0:half, 0:half] = r11 * jnp.concatenate([back0, back1], axis=1)
     r_ref[half:, 0:half] = zero
-    inv_ref[0:half, 0:half] = w11
+    inv_ref[0:half, 0:half] = w11 * left_row
     inv_ref[0:half, half:] = zero
 
     sum_grps(x1, own_x, grp_x, cell_x)
@@ -250,19 +272,24 @@
 
     for copy in c3:
         copy.wait_recv()
-    r12 = dot(w11, all_c[0:half, :], ((1,), (0,)), HIGHEST)
+    upper = all_c[half : half + quarter, :]
+    last = all_c[half + quarter : half + quarter + eighth, :]
+    last = jnp.concatenate([last[:, :quarter], last[:, quarter:]], axis=0)
+    row2, col2, back2 = scales(upper[:, :quarter])
+    row3, col3, back3 = scales(last)
+    right_row, back = jnp.concatenate([row2, row3], axis=1), jnp.concatenate([back2, back3], axis=1)
+    r12 = dot(w11, all_c[0:half, :] * left_col * right_row, ((1,), (0,)), HIGHEST)
     r21 = r12.T
     taken = dot(r21, r12, ((1,), (0,)), HIGHEST)
-    upper = all_c[half : half + quarter, :] - taken[:quarter]
-    last = all_c[half + quarter : half + quarter + eighth, :]
-    last = jnp.concatenate([last[:, :quarter], last[:, quarter:]], axis=0) - taken[quarter:, quarter:]
+    upper = upper * col2 * right_row - taken[:quarter]
+    last = last * col3 * row3 - taken[quarter:, quarter:]
     mixed = dot(r21, w11, ((1,), (0,)), HIGHEST)
-    r_ref[0:half, half:] = r12
+    r_ref[0:half, half:] = r12 * back
     r_00, w_00 = factor_base(upper[:, :quarter], ones_ref)
     r22, w22 = extend(r_00, w_00, upper[:, quarter:], last, ones_ref)
-    r_ref[half:, half:] = r22
-    inv_ref[half:, 0:half] = -dot(w22, mixed, ((1,), (0,)), HIGHEST)
-    inv_ref[half:, half:] = w22
+    r_ref[half:, half:] = r22 * back
+    inv_ref[half:, 0:half] = -dot(w22, mixed, ((1,), (0,)), HIGHEST) * left_row
+    inv_ref[half:, half:] = w22 * right_row
     cross_ref[...] = sum_slots(x2, cell_x)
     for copy in started:
         copy.wait_send()
@@ -318,16 +345,16 @@
 
 
 def basis_kernel(
-    r_in, inv_ref, cross_ref, sketch_ref, r_out, basis_hbm, proj_ref, basis_ref, store_sems,
+    r_in, inv_ref, cross_ref, sketch_ref, r_hbm, basis_hbm, proj_ref, basis_ref, r_sem, store_sems,
 ):
     steps = chunks_of(sketch_ref.shape[0], BASIS_STEP)
     half = cross_ref.shape[1]
     days = cross_ref.shape[0] // 2
-    r_out[...] = r_in[...]
+    stores = [pltpu.make_async_copy(r_in, r_hbm, r_sem)]
+    stores[0].start()
     whole = inv_ref[...]
     high = whole.astype(jnp.bfloat16)
     low = (whole - high.astype(jnp.float32)).astype(jnp.bfloat16)
-    stores = []
     for i, rows in enumerate(steps):
         part = sketch_ref[rows, :]
         exact = dot(part, high, ((1,), (1,))) + dot(part, low, ((1,), (1,)))
@@ -356,9 +383,10 @@
             jax.ShapeDtypeStruct((days // grps, k // cells), jnp.float32),
         ),
         in_specs=[vmem] * 4,
-        out_specs=(vmem, hbm, vmem),
+        out_specs=(hbm, hbm, vmem),
         scratch_shapes=[
             pltpu.VMEM(sketch.shape, jnp.bfloat16),
+            pltpu.SemaphoreType.DMA,
             pltpu.SemaphoreType.DMA((steps,)),
         ],
         compiler_params=pltpu.CompilerParams(vmem_limit_bytes=VMEM_LIMIT),

time: 26 us -> 25.5 us (0.981)
  Pallas kernels: 25.2 us -> 24.7 us
    pallas_call x1, Pallas kernels: 22.6 us -> 22.2 us  [factored(): pl.pallas_call(functools.partial(factor_kernel, cells, grps), out_shape=(...]
where the time goes in v4:
time: 25.5 us; the launch traced here: 25.3 us
  Pallas kernels  24.7 us (97%)
  between operations  0.64 us (3%)
    pallas_call x1, Pallas kernels, factored(): pl.pallas_call(functools.partial(factor_kernel, cells, grps), out_shape=(...  22.2 us
    pallas_call x1, Pallas kernels, local(): pl.pallas_call(basis_kernel, out_shape=(jax.ShapeDtypeStruct((k, k), jnp....  2.53 us

profile of v4, /device:TPU:0, one launch (start us, length us, event | category | flops | bytes accessed | tf_op | source)
XLA Modules:
  0.0 25.3 jit_solution(10075017352507322312)
XLA Ops:
  0.6 22.2 %reduce_and_factor.1 = (f32[256,256]{1,0:T(8,128)S(1)}, f32[256,256]{1,0:T(8,128)S(1)}, f32[64,128]{1,0:T(8,128)S(1)}, bf16[3072,256]{1,0:T(8,128)(2,1)S(1)}) custom-call(bf16[3072,256]{1,0:T(8,128)(2,1)} %sketch_hbm.1, bf16[3072,128]{1,0:T(8,128)(2,1)} %slab_hbm.1), custom_call_target="tpu_custom_call" | custom-call | tf_op jit(solution)/shard_map/reduce_and_factor/pallas_call | solution.py:319
  22.8 2.5 %basis.1 = (f32[256,256]{1,0:T(8,128)}, bf16[3072,256]{1,0:T(8,128)(2,1)}, f32[32,64]{1,0:T(8,128)}) custom-call(f32[256,256]{1,0:T(8,128)S(1)} %get-tuple-element.10.r_in, f32[256,256]{1,0:T(8,128)S(1)} %get-tuple-element.11.inv_ref, f32[64,128]{1,0:T(8,128)S(1)} %get-tuple-element.12.cross_ref, bf16[3072,256]{1,0:T(8,128)(2,1)S(1)} %get-tuple-element.13.sketch_ref), custom_call_target="tpu_custom_call" | custom-call | tf_op jit(solution)/shard_map/basis/pallas_call | solution.py:378

commit v5 on v4

--- a/solution.py
+++ b/solution.py
@@ -52,6 +52,7 @@
     wide = jnp.concatenate([block, eye.astype(jnp.float32)], axis=1)
     m = [wide[q * SUB : (q + 1) * SUB, :] for q in range(tiles)]
     done = []
+    ahead = None
 
     def row(x, j):
         return jnp.broadcast_to(x[j : j + 1, :], shape)
@@ -61,7 +62,12 @@
 
     for p in range(tiles):
         t = m[p]
-        c = [col(t, p * SUB + i) * ones for i in range(SUB)]
+        c = [col(t, p * SUB + i) * ones for i in range(0 if ahead is None else 2, SUB)]
+        c = c if ahead is None else ahead + c
+        after = m[p + 1] if p + 1 < tiles else None
+        if after is not None:
+            e = [col(after, p * SUB + i) * ones for i in range(SUB)]
+            ahead = [col(after, (p + 1) * SUB + i) * ones for i in range(2)]
         corner = [row(c[0], 0), row(c[1], 0), row(c[1], 1)]
         r = jnp.zeros(shape, jnp.float32)
         for j in range(0, SUB, 2):
@@ -77,15 +83,20 @@
             t_j, t_k = row(t, j), row(t, k)
             r = jnp.where(at_j, t_j * root_a, jnp.where(at_k, (t_k * a - t_j * b) * (root_a * root), r))
             t = jnp.where(pair, 0.0, t) - (f_j * t_j + f_k * t_k) * inv
+            if after is not None:
+                n_j, n_k = e[j] * d - e[k] * b, e[k] * a - e[j] * b
+                ahead = [x - (n_j * row(e[j], i) + n_k * row(e[k], i)) * inv for i, x in enumerate(ahead)]
             if k + 1 < SUB:
                 s_j = {i: row(c[i], j) for i in range(k + 1, SUB)}
                 s_k = {i: row(c[i], k) for i in range(k + 1, SUB)}
-                e, g = k + 1, k + 2
-                v = {h: (s_j[h] * d - s_k[h] * b, s_k[h] * a - s_j[h] * b) for h in (e, g)}
+                x, y = k + 1, k + 2
+                v = {h: (s_j[h] * d - s_k[h] * b, s_k[h] * a - s_j[h] * b) for h in (x, y)}
                 corner = [
-                    row(c[i], h) - (v[h][0] * s_j[i] + v[h][1] * s_k[i]) * inv for h, i in ((e, e), (e, g), (g, g))]
+                    row(c[i], h) - (v[h][0] * s_j[i] + v[h][1] * s_k[i]) * inv for h, i in ((x, x), (x, y), (y, y))]
                 for i in range(k + 1, SUB):
                     c[i] = jnp.where(pair, 0.0, c[i]) - (f_j * s_j[i] + f_k * s_k[i]) * inv
+                    if after is not None:
+                        e[i] = e[i] - (n_j * s_j[i] + n_k * s_k[i]) * inv
         done.append(jnp.where((lane >= sub + p * SUB), r, 0.0))
         if p + 1 < tiles:
             rows = [row(t, i) for i in range(SUB)]

time: 25.5 us -> 25.4 us (level)
  no operation moved by 1% of the time
where the time goes in v5:
time: 25.4 us; the launch traced here: 25.3 us
  Pallas kernels  24.6 us (97%)
  between operations  0.64 us (3%)
    pallas_call x1, Pallas kernels, factored(): pl.pallas_call(functools.partial(factor_kernel, cells, grps), out_shape=(...  22.1 us
    pallas_call x1, Pallas kernels, local(): pl.pallas_call(basis_kernel, out_shape=(jax.ShapeDtypeStruct((k, k), jnp....  2.52 us

profile of v5, /device:TPU:0, one launch (start us, length us, event | category | flops | bytes accessed | tf_op | source)
XLA Modules:
  0.0 25.3 jit_solution(767451574146318119)
XLA Ops:
  0.6 22.1 %reduce_and_factor.1 = (f32[256,256]{1,0:T(8,128)S(1)}, f32[256,256]{1,0:T(8,128)S(1)}, f32[64,128]{1,0:T(8,128)S(1)}, bf16[3072,256]{1,0:T(8,128)(2,1)S(1)}) custom-call(bf16[3072,256]{1,0:T(8,128)(2,1)} %sketch_hbm.1, bf16[3072,128]{1,0:T(8,128)(2,1)} %slab_hbm.1), custom_call_target="tpu_custom_call" | custom-call | tf_op jit(solution)/shard_map/reduce_and_factor/pallas_call | solution.py:330
  22.8 2.5 %basis.1 = (f32[256,256]{1,0:T(8,128)}, bf16[3072,256]{1,0:T(8,128)(2,1)}, f32[32,64]{1,0:T(8,128)}) custom-call(f32[256,256]{1,0:T(8,128)S(1)} %get-tuple-element.10.r_in, f32[256,256]{1,0:T(8,128)S(1)} %get-tuple-element.11.inv_ref, f32[64,128]{1,0:T(8,128)S(1)} %get-tuple-element.12.cross_ref, bf16[3072,256]{1,0:T(8,128)(2,1)S(1)} %get-tuple-element.13.sketch_ref), custom_call_target="tpu_custom_call" | custom-call | tf_op jit(solution)/shard_map/basis/pallas_call | solution.py:389

commit v6 on v5

--- a/solution.py
+++ b/solution.py
@@ -11,7 +11,7 @@
 CORES = 2
 VMEM_LIMIT = 20 * 2**20
 SUM_STEP = 768
-BASIS_STEP = 512
+BASIS_STEP = 384
 HIGHEST = lax.Precision.HIGHEST
 
 
@@ -147,7 +147,6 @@
         return loads
 
     sketch_loads = loading(sketch_hbm, sketch_ref, sketch_sems)
-    slab_loads = loading(slab_hbm, slab_ref, slab_sems)
     me_c = lax.axis_index("cell")
     me_g = lax.axis_index("grp")
     chips_x = grps // CORES
@@ -181,6 +180,7 @@
         pl.semaphore_signal(barrier, inc=1, device_id=peer, device_id_type=pl.DeviceIdType.MESH)
 
     gram = sums_over(sketch_ref, sketch_ref, sketch_loads)
+    slab_loads = loading(slab_hbm, slab_ref, slab_sems)
     eighth = quarter // 2
     own_a[...] = jnp.concatenate([gram[:eighth, :quarter], gram[eighth:quarter, :quarter]], axis=1)
     own_b[...] = jnp.concatenate([gram[:quarter, quarter:half], gram[quarter:half, quarter:half]], axis=1)

time: 25.4 us -> 25.1 us (0.988)
  Pallas kernels: 24.6 us -> 24.3 us
    pallas_call x1, Pallas kernels: 22.1 us -> 21.8 us  [factored(): pl.pallas_call(functools.partial(factor_kernel, cells, grps), out_shape=(...]
where the time goes in v6:
time: 25.1 us; the launch traced here: 25 us
  Pallas kernels  24.3 us (97%)
  between operations  0.64 us (3%)
    pallas_call x1, Pallas kernels, factored(): pl.pallas_call(functools.partial(factor_kernel, cells, grps), out_shape=(...  21.8 us
    pallas_call x1, Pallas kernels, local(): pl.pallas_call(basis_kernel, out_shape=(jax.ShapeDtypeStruct((k, k), jnp....  2.5 us

profile of v6, /device:TPU:0, one launch (start us, length us, event | category | flops | bytes accessed | tf_op | source)
XLA Modules:
  0.0 25.0 jit_solution(8544581285628740552)
XLA Ops:
  0.6 21.8 %reduce_and_factor.1 = (f32[256,256]{1,0:T(8,128)S(1)}, f32[256,256]{1,0:T(8,128)S(1)}, f32[64,128]{1,0:T(8,128)S(1)}, bf16[3072,256]{1,0:T(8,128)(2,1)S(1)}) custom-call(bf16[3072,256]{1,0:T(8,128)(2,1)} %sketch_hbm.1, bf16[3072,128]{1,0:T(8,128)(2,1)} %slab_hbm.1), custom_call_target="tpu_custom_call" | custom-call | tf_op jit(solution)/shard_map/reduce_and_factor/pallas_call | solution.py:330
  22.5 2.5 %basis.1 = (f32[256,256]{1,0:T(8,128)}, bf16[3072,256]{1,0:T(8,128)(2,1)}, f32[32,64]{1,0:T(8,128)}) custom-call(f32[256,256]{1,0:T(8,128)S(1)} %get-tuple-element.10.r_in, f32[256,256]{1,0:T(8,128)S(1)} %get-tuple-element.11.inv_ref, f32[64,128]{1,0:T(8,128)S(1)} %get-tuple-element.12.cross_ref, bf16[3072,256]{1,0:T(8,128)(2,1)S(1)} %get-tuple-element.13.sketch_ref), custom_call_target="tpu_custom_call" | custom-call | tf_op jit(solution)/shard_map/basis/pallas_call | solution.py:389
